TPU v7x, 32 devices: a whole 2x2x4 slice. The times are simulated.
32 devices in a mesh: dp: 8 (over y, x, core), tensor: 4 (over z).
Axes of the slice: x: 2, y: 2, z: 4, core: 2. Of those that a mesh axis runs over, the one named last changes fastest.
Arguments:
- hidden_in: bfloat16 [2, 8, 1024, 2048], P(None, None, ('dp', 'tensor')), may hold values from -6 to 6
- lengths: int32 [2, 8], replicated, may hold values from 1 to 1024, 6144 in all within a row
- dealing: int32 [2, 8], replicated, may hold values from 0 to 7, each once within a row
- cotangent: bfloat16 [2, 8, 1024, 2048], P(None, None, ('dp', 'tensor')), may hold values from -6 to 6
- attn_gain: bfloat16 [2048], P(('dp', 'tensor')), may hold values from 0.5 to 1.5
- attn_shift: bfloat16 [2048], P(('dp', 'tensor')), may hold values from -1.5 to 1.5
- ffn_gain: bfloat16 [2048], P(('dp', 'tensor')), may hold values from 0.5 to 1.5
- ffn_shift: bfloat16 [2048], P(('dp', 'tensor')), may hold values from -1.5 to 1.5
- qkv_weight: bfloat16 [2048, 8, 768], P('dp', 'tensor'), may hold values from -0.125 to 0.125
- qkv_bias: bfloat16 [8, 768], P('tensor', 'dp'), may hold values from -0.25 to 0.25
- dense_weight: bfloat16 [8, 256, 2048], P('tensor', 'dp'), may hold values from -1.5 to 1.5
- dense_bias: bfloat16 [2048], P(('dp', 'tensor')), may hold values from -1.5 to 1.5
- fc1_weight: bfloat16 [2048, 8192], P('dp', 'tensor'), may hold values from -0.125 to 0.125
- fc1_bias: bfloat16 [8, 1024], P('tensor', 'dp'), may hold values from -1.5 to 1.5
- fc2_weight: bfloat16 [8192, 2048], P('tensor', 'dp'), may hold values from -0.0625 to 0.0625
- fc2_bias: bfloat16 [2048], P(('dp', 'tensor')), may hold values from -1.5 to 1.5
Outputs:
- output: bfloat16 [2, 8, 1024, 2048], P(None, None, ('dp', 'tensor'))
- input_grad: bfloat16 [2, 8, 1024, 2048], P(None, None, ('dp', 'tensor'))
- attngain_grad: float32 [2048], P(('dp', 'tensor'))
- attnshift_grad: float32 [2048], P(('dp', 'tensor'))
- ffngain_grad: float32 [2048], P(('dp', 'tensor'))
- ffnshift_grad: float32 [2048], P(('dp', 'tensor'))
- qkvweight_grad: float32 [2048, 8, 768], P('dp', 'tensor')
- qkvbias_grad: float32 [8, 768], P('tensor', 'dp')
- denseweight_grad: float32 [8, 256, 2048], P('tensor', 'dp')
- densebias_grad: float32 [2048], P(('dp', 'tensor'))
- fc1weight_grad: float32 [2048, 8192], P('dp', 'tensor')
- fc1bias_grad: float32 [8, 1024], P('tensor', 'dp')
- fc2weight_grad: float32 [8192, 2048], P('tensor', 'dp')
- fc2bias_grad: float32 [2048], P(('dp', 'tensor'))
Inputs may be any that keep to these rules, and one draw needn't show every extreme that they name: lengths[m, j] belongs to the sequence in input slot dealing[m, j]; in each micro-batch the lengths sum to 6144 and the longest is 1024. Each row of dealing holds every slot number once.
All inputs are finite; a program needn't handle non-finite values.
Results may differ from a plain program's by a relative error of at most 0.013.
Values may be sent and summed in bfloat16 or wider, within the bound.
No kernel may reach another device: no remote copies, remote signals or barrier semaphores. Data moves between devices by JAX's collectives and lax.ppermute only.
A program may use at most 320 MiB of HBM per device.

v0:
```python
import math
import jax
import jax.numpy as jnp
from jax import lax
from jax.sharding import PartitionSpec as P

HD = 256
ROT = 64
EPSILON = 1e-05
ROPE_BASE = 10000.0
NEG_FILL = -1e30
SQRT_HALF = 0.7071067811865476
INV_ROOT_TWO_PI = 0.3989422804014327


def normalize(residual, gain, shift):
    centred = residual - jnp.mean(residual, axis=-1, keepdims=True)
    scaling = lax.rsqrt(jnp.mean(centred * centred, axis=-1, keepdims=True) + EPSILON)
    unit_rows = centred * scaling
    return (unit_rows * gain + shift, unit_rows, scaling)


def norm_back(grad_out, unit_rows, scaling, gain):
    grad_unit = grad_out * gain
    return scaling * (
        grad_unit
        - jnp.mean(grad_unit, axis=-1, keepdims=True)
        - unit_rows * jnp.mean(grad_unit * unit_rows, axis=-1, keepdims=True)
    )


def angles(positions):
    freqs = jnp.exp(jnp.arange(ROT // 2, dtype=jnp.float32) * (-2.0 * math.log(ROPE_BASE) / ROT))
    phases = positions.astype(jnp.float32)[:, None] * freqs[None, :]
    return (jnp.cos(phases), jnp.sin(phases))


def rotate(heads, cosines, sines):
    half_rot = ROT // 2
    lead_part = heads[..., :half_rot]
    trail_part = heads[..., half_rot:ROT]
    cos_rows = cosines[:, None, :]
    sin_rows = sines[:, None, :]
    return jnp.concatenate(
        [
            lead_part * cos_rows - trail_part * sin_rows,
            trail_part * cos_rows + lead_part * sin_rows,
            heads[..., ROT:],
        ],
        axis=-1,
    )


def take_slots(table, order):
    return jnp.take(table, order, axis=0)


def per_device(
    hidden_in,
    lengths,
    dealing,
    cotangent,
    attn_gain,
    attn_shift,
    ffn_gain,
    ffn_shift,
    qkv_weight,
    qkv_bias,
    dense_weight,
    dense_bias,
    fc1_weight,
    fc1_bias,
    fc2_weight,
    fc2_bias,
):
    n_tensor = lax.axis_size("tensor")
    n_data = lax.axis_size("dp")
    group_index = lax.axis_index("dp")
    micro_count, seq_count, piece_rows, width = hidden_in.shape
    local_rows = n_data * piece_rows
    seq_rows = n_tensor * local_rows
    block_rows = min(512, seq_rows)
    block_count = seq_rows // block_rows
    scale = 1.0 / math.sqrt(HD)
    sent_in = jax.vmap(take_slots)(hidden_in, dealing)
    sent_grad = jax.vmap(take_slots)(cotangent, dealing)
    got_in, got_grad = (
        lax.all_to_all(sent_in, "dp", split_axis=1, concat_axis=2, tiled=True),
        lax.all_to_all(sent_grad, "dp", split_axis=1, concat_axis=2, tiled=True),
    )
    small = (
        lax.all_gather(attn_gain, ("dp", "tensor"), axis=0, tiled=True),
        lax.all_gather(attn_shift, ("dp", "tensor"), axis=0, tiled=True),
        lax.all_gather(ffn_gain, ("dp", "tensor"), axis=0, tiled=True),
        lax.all_gather(ffn_shift, ("dp", "tensor"), axis=0, tiled=True),
        lax.all_gather(dense_bias, ("dp", "tensor"), axis=0, tiled=True),
        lax.all_gather(fc2_bias, ("dp", "tensor"), axis=0, tiled=True),
    )
    gain_one, shift_one, gain_two, shift_two, dense_shift, fc2_shift = [
        piece.astype(jnp.float32) for piece in small
    ]
    shard_set = (qkv_weight, qkv_bias, dense_weight, fc1_weight, fc1_bias, fc2_weight)

    def current_set():
        return (
            lax.all_gather(shard_set[0], "dp", axis=0, tiled=True),
            lax.all_gather(shard_set[1], "dp", axis=1, tiled=True),
            lax.all_gather(shard_set[2], "dp", axis=1, tiled=True),
            lax.all_gather(shard_set[3], "dp", axis=0, tiled=True),
            lax.all_gather(shard_set[4], "dp", axis=1, tiled=True),
            lax.all_gather(shard_set[5], "dp", axis=1, tiled=True),
        )

    row_ids = jnp.arange(seq_rows, dtype=jnp.int32)
    part_ids = row_ids // local_rows
    within = row_ids % local_rows
    positions = (within // piece_rows * n_tensor + part_ids) * piece_rows + within % piece_rows
    cosines, sines = angles(positions)
    my_lengths = lax.dynamic_index_in_dim(lengths, group_index, axis=1, keepdims=False)
    starts = jnp.arange(block_count, dtype=jnp.int32) * block_rows
    heads_here = qkv_weight.shape[1]
    units_here = fc1_weight.shape[1]
    weight_zero = (
        jnp.zeros((width, heads_here, 3 * HD), jnp.float32),
        jnp.zeros((heads_here, 3 * HD), jnp.float32),
        jnp.zeros((heads_here, HD, width), jnp.float32),
        jnp.zeros((width, units_here), jnp.float32),
        jnp.zeros((heads_here, units_here // heads_here), jnp.float32),
        jnp.zeros((units_here, width), jnp.float32),
    )
    small_zero = tuple((jnp.zeros((width,), jnp.float32) for index_slot in range(6)))

    def micro_step(totals, item):
        weight_totals, small_totals = totals
        rows_in, rows_grad, seq_length = item
        qkv_full, qkv_shift, dense_full, fc1_full, fc1_shift, fc2_full = current_set()
        residual = rows_in.astype(jnp.float32)
        normed_one, unit_one, scale_one = normalize(residual, gain_one, shift_one)
        normed_two = unit_one * gain_two + shift_two
        full_one, full_two = (
            lax.all_gather(normed_one.astype(jnp.bfloat16), "tensor", axis=0, tiled=True),
            lax.all_gather(normed_two.astype(jnp.bfloat16), "tensor", axis=0, tiled=True),
        )
        projected = jnp.einsum(
            "ld,dhe->lhe", full_one, qkv_full, preferred_element_type=jnp.float32
        ) + qkv_shift.astype(jnp.float32)
        queries = rotate(projected[..., :HD], cosines, sines).astype(jnp.bfloat16)
        key_rows = rotate(projected[..., HD : 2 * HD], cosines, sines).astype(jnp.bfloat16)
        value_rows = projected[..., 2 * HD :].astype(jnp.bfloat16)

        def mask_for(row_start):
            q_pos = lax.dynamic_slice_in_dim(positions, row_start, block_rows, 0)
            return (positions[None, :] <= q_pos[:, None]) & (positions[None, :] < seq_length)

        def attend(row_start):
            q_block = lax.dynamic_slice_in_dim(queries, row_start, block_rows, 0)
            scores = (
                jnp.einsum("qhe,khe->hqk", q_block, key_rows, preferred_element_type=jnp.float32)
                * scale
            )
            scores = jnp.where(mask_for(row_start)[None], scores, NEG_FILL)
            row_max = jnp.max(scores, axis=-1, keepdims=True)
            expo = jnp.exp(scores - row_max)
            row_sum = jnp.sum(expo, axis=-1, keepdims=True)
            softmax_w = (expo / row_sum).astype(jnp.bfloat16)
            mixed_block = jnp.einsum(
                "hqk,khe->qhe", softmax_w, value_rows, preferred_element_type=jnp.float32
            ).astype(jnp.bfloat16)
            return (mixed_block, (row_max + jnp.log(row_sum))[..., 0])

        mixed_blocks, lse_blocks = lax.map(attend, starts)
        mixed = mixed_blocks.reshape(seq_rows, heads_here, HD)
        attn_part = jnp.einsum("lhe,hed->ld", mixed, dense_full, preferred_element_type=jnp.float32)
        preact = jnp.dot(
            full_two, fc1_full, preferred_element_type=jnp.float32
        ) + fc1_shift.reshape(-1).astype(jnp.float32)
        activation = jax.nn.gelu(preact, approximate=False).astype(jnp.bfloat16)
        ffn_part = jnp.dot(activation, fc2_full, preferred_element_type=jnp.float32)
        branch = lax.psum_scatter(attn_part + ffn_part, "tensor", scatter_dimension=0, tiled=True)
        output_rows = (residual + branch + dense_shift + fc2_shift).astype(jnp.bfloat16)
        back_set = current_set()
        grad_full = lax.all_gather(rows_grad, "tensor", axis=0, tiled=True)
        grad_dense = jnp.einsum("lhe,ld->hed", mixed, grad_full, preferred_element_type=jnp.float32)
        grad_mixed = jnp.einsum(
            "ld,hed->lhe", grad_full, back_set[2], preferred_element_type=jnp.float32
        ).astype(jnp.bfloat16)
        grad_fc2 = jnp.einsum(
            "lf,ld->fd", activation, grad_full, preferred_element_type=jnp.float32
        )
        grad_act = jnp.einsum(
            "ld,fd->lf", grad_full, back_set[5], preferred_element_type=jnp.float32
        )
        normal_cdf = 0.5 * (1.0 + lax.erf(preact * SQRT_HALF))
        slope = normal_cdf + preact * jnp.exp(-0.5 * preact * preact) * INV_ROOT_TWO_PI
        grad_pre = (grad_act * slope).astype(jnp.bfloat16)
        grad_fc1 = jnp.einsum("ld,lf->df", full_two, grad_pre, preferred_element_type=jnp.float32)
        grad_fc1b = jnp.sum(grad_pre.astype(jnp.float32), axis=0).reshape(
            heads_here, units_here // heads_here
        )
        grad_second = jnp.einsum(
            "lf,df->ld", grad_pre, back_set[3], preferred_element_type=jnp.float32
        )

        def back_block(carry, block_item):
            key_grad, value_grad = carry
            row_start, lse_block = block_item
            q_block = lax.dynamic_slice_in_dim(queries, row_start, block_rows, 0)
            grad_block = lax.dynamic_slice_in_dim(grad_mixed, row_start, block_rows, 0)
            scores = (
                jnp.einsum("qhe,khe->hqk", q_block, key_rows, preferred_element_type=jnp.float32)
                * scale
            )
            scores = jnp.where(mask_for(row_start)[None], scores, NEG_FILL)
            softmax_f = jnp.exp(scores - lse_block[..., None])
            softmax_w = softmax_f.astype(jnp.bfloat16)
            value_grad = value_grad + jnp.einsum(
                "hqk,qhe->khe", softmax_w, grad_block, preferred_element_type=jnp.float32
            )
            grad_soft = jnp.einsum(
                "qhe,khe->hqk", grad_block, value_rows, preferred_element_type=jnp.float32
            )
            grad_scores = (
                softmax_f * (grad_soft - jnp.sum(softmax_f * grad_soft, axis=-1, keepdims=True))
            ).astype(jnp.bfloat16)
            query_part = (
                jnp.einsum(
                    "hqk,khe->qhe", grad_scores, key_rows, preferred_element_type=jnp.float32
                )
                * scale
            )
            key_grad = (
                key_grad
                + jnp.einsum(
                    "hqk,qhe->khe", grad_scores, q_block, preferred_element_type=jnp.float32
                )
                * scale
            )
            return ((key_grad, value_grad), query_part)

        zero_heads = jnp.zeros((seq_rows, heads_here, HD), jnp.float32)
        (key_grad, value_grad), query_parts = lax.scan(
            back_block, (zero_heads, zero_heads), (starts, lse_blocks)
        )
        query_grad = query_parts.reshape(seq_rows, heads_here, HD)
        grad_qkv = jnp.concatenate(
            [rotate(query_grad, cosines, -sines), rotate(key_grad, cosines, -sines), value_grad],
            axis=-1,
        ).astype(jnp.bfloat16)
        grad_qkvw = jnp.einsum(
            "ld,lhe->dhe", full_one, grad_qkv, preferred_element_type=jnp.float32
        )
        grad_qkvb = jnp.sum(grad_qkv.astype(jnp.float32), axis=0)
        grad_first = jnp.einsum(
            "lhe,dhe->ld", grad_qkv, back_set[0], preferred_element_type=jnp.float32
        )
        upstream = rows_grad.astype(jnp.float32)
        upstream_sum = jnp.sum(upstream, axis=0)
        norm_one, norm_two = (
            lax.psum_scatter(grad_first, "tensor", scatter_dimension=0, tiled=True),
            lax.psum_scatter(grad_second, "tensor", scatter_dimension=0, tiled=True),
        )
        input_rows = (
            upstream
            + norm_back(norm_one, unit_one, scale_one, gain_one)
            + norm_back(norm_two, unit_one, scale_one, gain_two)
        ).astype(jnp.bfloat16)
        small_terms = (
            jnp.sum(norm_one * unit_one, axis=0),
            jnp.sum(norm_one, axis=0),
            jnp.sum(norm_two * unit_one, axis=0),
            jnp.sum(norm_two, axis=0),
            upstream_sum,
            upstream_sum,
        )
        weight_terms = (grad_qkvw, grad_qkvb, grad_dense, grad_fc1, grad_fc1b, grad_fc2)
        new_weights = tuple((total + term for total, term in zip(weight_totals, weight_terms)))
        new_small = tuple((total + term for total, term in zip(small_totals, small_terms)))
        return ((new_weights, new_small), (output_rows, input_rows))

    (weight_totals, small_totals), (output_rows, input_rows) = lax.scan(
        micro_step, (weight_zero, small_zero), (got_in[:, 0], got_grad[:, 0], my_lengths)
    )
    weight_sums = (
        lax.psum_scatter(
            weight_totals[0].astype(jnp.bfloat16), "dp", scatter_dimension=0, tiled=True
        ).astype(jnp.float32),
        lax.psum_scatter(
            weight_totals[1].astype(jnp.bfloat16), "dp", scatter_dimension=1, tiled=True
        ).astype(jnp.float32),
        lax.psum_scatter(
            weight_totals[2].astype(jnp.bfloat16), "dp", scatter_dimension=1, tiled=True
        ).astype(jnp.float32),
        lax.psum_scatter(
            weight_totals[3].astype(jnp.bfloat16), "dp", scatter_dimension=0, tiled=True
        ).astype(jnp.float32),
        lax.psum_scatter(
            weight_totals[4].astype(jnp.bfloat16), "dp", scatter_dimension=1, tiled=True
        ).astype(jnp.float32),
        lax.psum_scatter(
            weight_totals[5].astype(jnp.bfloat16), "dp", scatter_dimension=1, tiled=True
        ).astype(jnp.float32),
    )
    small_sums = lax.psum_scatter(small_totals, ("dp", "tensor"), scatter_dimension=0, tiled=True)
    back_out, back_grad = (
        lax.all_to_all(output_rows[:, None], "dp", split_axis=2, concat_axis=1, tiled=True),
        lax.all_to_all(input_rows[:, None], "dp", split_axis=2, concat_axis=1, tiled=True),
    )
    slot_ids = jnp.arange(seq_count, dtype=jnp.int32)
    inverse = jnp.sum(
        jnp.where(dealing[:, :, None] == slot_ids[None, None, :], slot_ids[None, :, None], 0),
        axis=1,
    )
    output = jax.vmap(take_slots)(back_out, inverse)
    input_grad = jax.vmap(take_slots)(back_grad, inverse)
    return (
        output,
        input_grad,
        small_sums[0],
        small_sums[1],
        small_sums[2],
        small_sums[3],
        weight_sums[0],
        weight_sums[1],
        weight_sums[2],
        small_sums[4],
        weight_sums[3],
        weight_sums[4],
        weight_sums[5],
        small_sums[5],
    )


def solution(mesh):
    return jax.shard_map(
        per_device,
        mesh=mesh,
        in_specs=(
            P(None, None, ("dp", "tensor"), None),
            P(),
            P(),
            P(None, None, ("dp", "tensor"), None),
            P(("dp", "tensor")),
            P(("dp", "tensor")),
            P(("dp", "tensor")),
            P(("dp", "tensor")),
            P("dp", "tensor", None),
            P("tensor", "dp"),
            P("tensor", "dp", None),
            P(("dp", "tensor")),
            P("dp", "tensor"),
            P("tensor", "dp"),
            P("tensor", "dp"),
            P(("dp", "tensor")),
        ),
        out_specs=(
            P(None, None, ("dp", "tensor"), None),
            P(None, None, ("dp", "tensor"), None),
            P(("dp", "tensor")),
            P(("dp", "tensor")),
            P(("dp", "tensor")),
            P(("dp", "tensor")),
            P("dp", "tensor", None),
            P("tensor", "dp"),
            P("tensor", "dp", None),
            P(("dp", "tensor")),
            P("dp", "tensor"),
            P("tensor", "dp"),
            P("tensor", "dp"),
            P(("dp", "tensor")),
        ),
        check_vma=False,
    )
```

profile of v0, /device:TPU:0, one launch (start us, length us, event | category | flops | bytes accessed | tf_op | source)
XLA Modules:
  0.0 2300.3 jit_solution(938326112984021490)
XLA Ops:
  28.8 23.3 %all-to-all-done = bf16[2,8,32,2048]{3,2,0,1:T(8,128)(2,1)S(1)} async-done(((bf16[2,8,32,2048]{3,2,0,1:T(8,128)(2,1)}), bf16[2,8,32,2048]{3,2,0,1:T(8,128)(2,1)S(1)}, u32[]{:S(2)}, u32[]{:S(2)}) %all-to-all-start) | async-done | bytes 2097184 | tf_op jit(solution)/shard_map/all_to_all | solution.py:88
  58.2 58.6 %all-reduce.14 = (bf16[2048]{0:T(1024)(128)(2,1)S(1)}, bf16[2048]{0:T(1024)(128)(2,1)S(1)}, bf16[2048]{0:T(1024)(128)(2,1)S(1)}, bf16[2048]{0:T(1024)(128)(2,1)S...) all-reduce(bf16[2048]{0:T(1024)(128)(2,1)S(1)} %dynamic-update-slic, ...), channel_id=1, replica_groups=mesh['dp'=8,'tensor'=4] {'dp','tensor'}, use_global_device_ids=true, to_apply=%add | all-reduce | flops 12288 | bytes 49152
  127.4 1772.7 %while.89 = (s32[]{:T(128)}, f32[2048,2,768]{2,0,1:T(8,128)}, f32[2,768]{1,0:T(2,128)}, f32[2,256,2048]{2,1,0:T(8,128)}, f32[2048,2048]{1,0:T(8,128)}, /*index=5...) while((s32[]{:T(128)}, f32[2048,2,768]{2,0,1:T(8,128)}, ...), condition=%wide.region_24.26_spmd.clone.clone.clone.clone, body=%wide.region_0.25_spmd.clone.clone.clone.clone.sunk | while | flops 81338195968 | bytes 859343296 | solution.py:280
  157.5 82.4 %all-gather.26.cloned.1.call-done = bf16[1,1024,2048]{2,1,0:T(8,128)(2,1)} async-done(((bf16[1,256,2048]{2,1,0:T(8,128)(2,1)}), bf16[1,1024,2048]{2,1,0:T(8,128)(2,1)}) %all-gather.26.cloned.1.call-update) | async-done | bytes 4194320 | tf_op jit(solution)/shard_map/while/body/eval_jaxpr/all_gather | solution.py:182
  246.1 74.7 %all-gather.22.cloned.1.call-done = bf16[1024,2048]{1,0:T(8,128)(2,1)} async-done(((bf16[256,2048]{1,0:T(8,128)(2,1)}), bf16[1024,2048]{1,0:T(8,128)(2,1)}) %all-gather.22.cloned.1.call-update) | async-done | bytes 4194320 | tf_op jit(solution)/shard_map/while/body/eval_jaxpr/all_gather | solution.py:141
  320.8 47.0 %all-gather.20.cloned.1.call-done = bf16[2048,2,768]{0,2,1:T(8,128)(2,1)} async-done(((bf16[256,2,768]{0,2,1:T(8,128)(2,1)}), bf16[2048,2,768]{0,2,1:T(8,128)(2,1)}) %all-gather.20.cloned.1.call-update) | async-done | bytes 6291472 | tf_op jit(solution)/shard_map/while/body/eval_jaxpr/all_gather | solution.py:106
  405.0 87.3 %while.91 = (s32[]{:T(128)}, f32[1024,2,256]{0,2,1:T(8,128)}, f32[1024,2,256]{0,2,1:T(8,128)}, f32[2,512,2,256]{1,0,3,2:T(2,128)}, s32[2]{0:T(128)S(1)}, /*index...) while((s32[]{:T(128)}, f32[1024,2,256]{0,2,1:T(8,128)}, ...), condition=%wide.region_9.10_spmd.clone.clone, body=%wide.region_7.9_spmd.clone.clone.sunk | while | flops 2704015360 | bytes 111194568 | solution.py:241
  538.0 31.3 %fusion.250 = (bf16[1024,2048]{1,0:T(8,128)(2,1)}, f32[1024,2048]{1,0:T(8,128)}) fusion(f32[2048]{0:T(1024)S(1)} %bitcast.334, bf16[1024,2048]{1,0:T(8,128)(2,1)} %all-gather.28.cloned.1.call-done, bf16[2048,2048]{1,0:T(8,128)(2,1)} %all-gather.30.cloned.1.call-done), kind=kOutput, calls=%fused_computation.67.clone.1 | convolution fusion | flops 8728346624 | bytes 25174016 | tf_op jit(solution)/shard_map/while/body/eval_jaxpr/dot_general | solution.py:174
  665.1 44.9 %reduce-scatter.25.cloned.1.call-done = f32[256,2048]{1,0:T(8,128)} async-done(((f32[1024,2048]{1,0:T(8,128)}), f32[256,2048]{1,0:T(8,128)}) %reduce-scatter.25.cloned.1.call-update) | async-done | bytes 2097168 | tf_op jit(solution)/shard_map/while/body/eval_jaxpr/reduce_scatter | solution.py:259
  710.0 147.6 %reduce-scatter.23.cloned.1.call-done = f32[256,2048]{1,0:T(8,128)} async-done(((f32[1024,2048]{1,0:T(8,128)}), f32[256,2048]{1,0:T(8,128)}) %reduce-scatter.23.cloned.1.call-update) | async-done | bytes 2097168 | tf_op jit(solution)/shard_map/while/body/eval_jaxpr/reduce_scatter | solution.py:260
  861.8 143.2 %reduce-scatter.27.cloned.1.call-done = f32[256,2048]{1,0:T(8,128)} async-done(((f32[1024,2048]{1,0:T(8,128)}), f32[256,2048]{1,0:T(8,128)}) %reduce-scatter.27.cloned.1.call-update) | async-done | bytes 2097168 | tf_op jit(solution)/shard_map/while/body/eval_jaxpr/reduce_scatter | solution.py:179
  1041.8 82.2 %all-gather.26.cloned.1.call-done = bf16[1,1024,2048]{2,1,0:T(8,128)(2,1)} async-done(((bf16[1,256,2048]{2,1,0:T(8,128)(2,1)}), bf16[1,1024,2048]{2,1,0:T(8,128)(2,1)}) %all-gather.26.cloned.1.call-update) | async-done | bytes 4194320 | tf_op jit(solution)/shard_map/while/body/eval_jaxpr/all_gather | solution.py:182
  1130.2 74.7 %all-gather.22.cloned.1.call-done = bf16[1024,2048]{1,0:T(8,128)(2,1)} async-done(((bf16[256,2048]{1,0:T(8,128)(2,1)}), bf16[1024,2048]{1,0:T(8,128)(2,1)}) %all-gather.22.cloned.1.call-update) | async-done | bytes 4194320 | tf_op jit(solution)/shard_map/while/body/eval_jaxpr/all_gather | solution.py:141
  1204.9 47.0 %all-gather.20.cloned.1.call-done = bf16[2048,2,768]{0,2,1:T(8,128)(2,1)} async-done(((bf16[256,2,768]{0,2,1:T(8,128)(2,1)}), bf16[2048,2,768]{0,2,1:T(8,128)(2,1)}) %all-gather.20.cloned.1.call-update) | async-done | bytes 6291472 | tf_op jit(solution)/shard_map/while/body/eval_jaxpr/all_gather | solution.py:106
  1289.2 87.3 %while.91 = (s32[]{:T(128)}, f32[1024,2,256]{0,2,1:T(8,128)}, f32[1024,2,256]{0,2,1:T(8,128)}, f32[2,512,2,256]{1,0,3,2:T(2,128)}, s32[2]{0:T(128)S(1)}, /*index...) while((s32[]{:T(128)}, f32[1024,2,256]{0,2,1:T(8,128)}, ...), condition=%wide.region_9.10_spmd.clone.clone, body=%wide.region_7.9_spmd.clone.clone.sunk | while | flops 2704015360 | bytes 111194568 | solution.py:241
  1422.2 31.4 %fusion.250 = (bf16[1024,2048]{1,0:T(8,128)(2,1)}, f32[1024,2048]{1,0:T(8,128)}) fusion(f32[2048]{0:T(1024)S(1)} %bitcast.334, bf16[1024,2048]{1,0:T(8,128)(2,1)} %all-gather.28.cloned.1.call-done, bf16[2048,2048]{1,0:T(8,128)(2,1)} %all-gather.30.cloned.1.call-done), kind=kOutput, calls=%fused_computation.67.clone.1 | convolution fusion | flops 8728346624 | bytes 25174016 | tf_op jit(solution)/shard_map/while/body/eval_jaxpr/dot_general | solution.py:174
  1559.4 34.4 %reduce-scatter.25.cloned.1.call-done = f32[256,2048]{1,0:T(8,128)} async-done(((f32[1024,2048]{1,0:T(8,128)}), f32[256,2048]{1,0:T(8,128)}) %reduce-scatter.25.cloned.1.call-update) | async-done | bytes 2097168 | tf_op jit(solution)/shard_map/while/body/eval_jaxpr/reduce_scatter | solution.py:259
  1593.8 147.6 %reduce-scatter.23.cloned.1.call-done = f32[256,2048]{1,0:T(8,128)} async-done(((f32[1024,2048]{1,0:T(8,128)}), f32[256,2048]{1,0:T(8,128)}) %reduce-scatter.23.cloned.1.call-update) | async-done | bytes 2097168 | tf_op jit(solution)/shard_map/while/body/eval_jaxpr/reduce_scatter | solution.py:260
  1745.6 143.2 %reduce-scatter.27.cloned.1.call-done = f32[256,2048]{1,0:T(8,128)} async-done(((f32[1024,2048]{1,0:T(8,128)}), f32[256,2048]{1,0:T(8,128)}) %reduce-scatter.27.cloned.1.call-update) | async-done | bytes 2097168 | tf_op jit(solution)/shard_map/while/body/eval_jaxpr/reduce_scatter | solution.py:179
  1961.7 22.5 all-to-all-done.3
  1990.1 64.1 %all-reduce.13 = (f32[2048]{0:T(1024)S(1)}, f32[2048]{0:T(1024)S(1)}, f32[2048]{0:T(1024)S(1)}, f32[2048]{0:T(1024)S(1)}, f32[2048]{0:T(1024)S(1)}, /*index=5*/f32[2048]{0:T(1024)S(1)}) all-reduce(f32[2048]{0:T(1024)S(1)} %copy-done.33, f32[2048]{0:T(1024)S(1)} %copy-done.36, ...), channel_id=6, replica_groups=mesh['dp'=8,'tensor'=4] {'dp','tensor'}, use_global_device_ids=true, to_apply=%region_26.28.clone | all-reduce | flops 12288 | bytes 98304
  2077.5 62.7 %all-reduce.17.cloned.1.call-done = bf16[2048,2,768]{2,1,0:T(2,128)(2,1)} async-done(((bf16[2048,2,768]{2,1,0:T(2,128)(2,1)}), bf16[2048,2,768]{2,1,0:T(2,128)(2,1)}) %all-reduce.17.cloned.1.call-update) | async-done | bytes 6291472
  2143.0 72.0 %reduce-scatter.15.cloned.1.call-done = bf16[256,2048]{1,0:T(8,128)(2,1)} async-done(((bf16[2048,2048]{1,0:T(8,128)(2,1)}), bf16[256,2048]{1,0:T(8,128)(2,1)}) %reduce-scatter.15.cloned.1.call-update) | async-done | bytes 1048592 | tf_op jit(solution)/shard_map/reduce_scatter | solution.py:293
  2217.7 72.2 %reduce-scatter.17.cloned.1.call-done = bf16[2048,256]{1,0:T(8,128)(2,1)} async-done(((bf16[2048,2048]{1,0:T(8,128)(2,1)}), bf16[2048,256]{1,0:T(8,128)(2,1)}) %reduce-scatter.17.cloned.1.call-update) | async-done | bytes 1048592 | tf_op jit(solution)/shard_map/reduce_scatter | solution.py:299
  (643 shorter events, 786.0 us)
Async XLA Ops:
  128.5 111.3 %all-gather.26.cloned.1.call-start = ((), (), s32[]{:S(2)}) async-start(), calls=%async_computation.21 | async-start | bytes 5242880 | tf_op jit(solution)/shard_map/while/body/eval_jaxpr/all_gather | solution.py:182
  131.7 189.1 %all-gather.22.cloned.1.call-start = ((), (), s32[]{:S(2)}) async-start(), calls=%async_computation.19 | async-start | bytes 5242880 | tf_op jit(solution)/shard_map/while/body/eval_jaxpr/all_gather | solution.py:141
  135.4 232.4 %all-gather.20.cloned.1.call-start = ((), (), s32[]{:S(2)}) async-start(), calls=%async_computation.18 | async-start | bytes 7077888 | tf_op jit(solution)/shard_map/while/body/eval_jaxpr/all_gather | solution.py:106
  135.9 402.0 %all-gather.28.cloned.1.call-start = ((), (), s32[]{:S(2)}) async-start(), calls=%async_computation.22 | async-start | bytes 5242880 | tf_op jit(solution)/shard_map/while/body/eval_jaxpr/all_gather | solution.py:142
  136.5 401.5 %all-gather.30.cloned.1.call-start = ((), (), s32[]{:S(2)}) async-start(), calls=%async_computation.23 | async-start | bytes 9437184 | tf_op jit(solution)/shard_map/while/body/eval_jaxpr/all_gather | solution.py:109
  137.1 432.2 %all-gather.32.cloned.1.call-start = ((), (), s32[]{:S(2)}) async-start(), calls=%async_computation.24 | async-start | bytes 9437184 | tf_op jit(solution)/shard_map/while/body/eval_jaxpr/all_gather | solution.py:111
  137.9 572.1 %reduce-scatter.25.cloned.1.call-start = ((), (), s32[]{:S(2)}) async-start(), calls=%async_computation.26 | async-start | bytes 10485760 | tf_op jit(solution)/shard_map/while/body/eval_jaxpr/reduce_scatter | solution.py:259
  528.6 329.0 %reduce-scatter.23.cloned.1.call-start = ((), (), s32[]{:S(2)}) async-start(), calls=%async_computation.25 | async-start | bytes 10485760 | tf_op jit(solution)/shard_map/while/body/eval_jaxpr/reduce_scatter | solution.py:260
  599.9 405.1 %reduce-scatter.27.cloned.1.call-start = ((), (), s32[]{:S(2)}) async-start(), calls=%async_computation.27 | async-start | bytes 10485760 | tf_op jit(solution)/shard_map/while/body/eval_jaxpr/reduce_scatter | solution.py:179
  1011.1 112.9 %all-gather.26.cloned.1.call-start = ((), (), s32[]{:S(2)}) async-start(), calls=%async_computation.21 | async-start | bytes 5242880 | tf_op jit(solution)/shard_map/while/body/eval_jaxpr/all_gather | solution.py:182
  1014.3 190.6 %all-gather.22.cloned.1.call-start = ((), (), s32[]{:S(2)}) async-start(), calls=%async_computation.19 | async-start | bytes 5242880 | tf_op jit(solution)/shard_map/while/body/eval_jaxpr/all_gather | solution.py:141
  1018.0 233.9 %all-gather.20.cloned.1.call-start = ((), (), s32[]{:S(2)}) async-start(), calls=%async_computation.18 | async-start | bytes 7077888 | tf_op jit(solution)/shard_map/while/body/eval_jaxpr/all_gather | solution.py:106
  1018.5 403.6 %all-gather.28.cloned.1.call-start = ((), (), s32[]{:S(2)}) async-start(), calls=%async_computation.22 | async-start | bytes 5242880 | tf_op jit(solution)/shard_map/while/body/eval_jaxpr/all_gather | solution.py:142
  1019.1 403.0 %all-gather.30.cloned.1.call-start = ((), (), s32[]{:S(2)}) async-start(), calls=%async_computation.23 | async-start | bytes 9437184 | tf_op jit(solution)/shard_map/while/body/eval_jaxpr/all_gather | solution.py:109
  1019.7 433.8 %all-gather.32.cloned.1.call-start = ((), (), s32[]{:S(2)}) async-start(), calls=%async_computation.24 | async-start | bytes 9437184 | tf_op jit(solution)/shard_map/while/body/eval_jaxpr/all_gather | solution.py:111
  1020.3 573.5 %reduce-scatter.25.cloned.1.call-start = ((), (), s32[]{:S(2)}) async-start(), calls=%async_computation.26 | async-start | bytes 10485760 | tf_op jit(solution)/shard_map/while/body/eval_jaxpr/reduce_scatter | solution.py:259
  1412.7 328.7 %reduce-scatter.23.cloned.1.call-start = ((), (), s32[]{:S(2)}) async-start(), calls=%async_computation.25 | async-start | bytes 10485760 | tf_op jit(solution)/shard_map/while/body/eval_jaxpr/reduce_scatter | solution.py:260
  1484.0 404.8 %reduce-scatter.27.cloned.1.call-start = ((), (), s32[]{:S(2)}) async-start(), calls=%async_computation.27 | async-start | bytes 10485760 | tf_op jit(solution)/shard_map/while/body/eval_jaxpr/reduce_scatter | solution.py:179
  1900.2 157.4 %reduce-scatter.19.cloned.1.call-start = ((), (), s32[]{:S(2)}) async-start(), calls=%async_computation.15 | async-start | bytes 221184
  1901.8 157.2 %reduce-scatter.21.cloned.1.call-start = ((), (), s32[]{:S(2)}) async-start(), calls=%async_computation.16 | async-start | bytes 294912
  1903.5 172.0 %reduce-scatter.13.cloned.1.call-start = ((), (), s32[]{:S(2)}) async-start(), calls=%async_computation.12 | async-start | bytes 2359296 | tf_op jit(solution)/shard_map/reduce_scatter | solution.py:290
  1907.4 232.8 %all-reduce.17.cloned.1.call-start = ((), (), s32[]{:S(2)}) async-start(), calls=%async_computation.17 | async-start | bytes 12582912
  1929.4 285.5 %reduce-scatter.15.cloned.1.call-start = ((), (), s32[]{:S(2)}) async-start(), calls=%async_computation.13 | async-start | bytes 9437184 | tf_op jit(solution)/shard_map/reduce_scatter | solution.py:293
  1938.6 351.4 %reduce-scatter.17.cloned.1.call-start = ((), (), s32[]{:S(2)}) async-start(), calls=%async_computation.14 | async-start | bytes 9437184 | tf_op jit(solution)/shard_map/reduce_scatter | solution.py:299
  (146 other events, 7771.3 us)
Sparse Core Ops, SparseCore 0:
  130.6 26.9 all-gather.23
  159.1 80.7 all-gather.25
  241.5 79.2 all-gather.21
  322.5 45.1 all-gather.19
  369.7 80.7 all-gather.27
  452.3 52.9 all-gather.29
  507.1 55.9 all-gather.31
  565.5 144.4 reduce-scatter.24
  712.3 145.1 reduce-scatter.22
  859.8 145.1 reduce-scatter.26
  1013.1 28.6 all-gather.23
  1043.2 80.7 all-gather.25
  1125.6 79.2 all-gather.21
  1206.7 45.1 all-gather.19
  1253.9 80.7 all-gather.27
  1336.4 52.9 all-gather.29
  1391.1 55.9 all-gather.31
  1449.3 144.4 reduce-scatter.24
  1596.2 145.1 reduce-scatter.22
  1743.6 145.1 reduce-scatter.26
Sparse Core Ops, SparseCore 1:
  1904.2 34.2 reduce-scatter.18
  1942.3 34.7 reduce-scatter.20
  1980.2 51.9 reduce-scatter.12
  2035.8 104.3 all-reduce.16
  2143.6 71.2 reduce-scatter.14
  2218.8 71.1 reduce-scatter.16
where the time goes:
time: 2310 us; the launch traced here: 2300 us
  waiting for transfers between devices  1340 us (58%)
  matrix products  387 us (17%)
  local copies, waits for them, and re-layouts  238 us (10%)
  blocking collectives  159 us (7%)
  other arithmetic  111 us (5%)
  loops' own time  25.3 us (1%)
    reduce_scatter x2, waiting for transfers between devices, micro_step(): lax.psum_scatter(grad_second, 'tensor', scatter_dimension=0, tiled=True)  295 us
    reduce_scatter x2, waiting for transfers between devices, micro_step(): lax.psum_scatter(attn_part + ffn_part, 'tensor', scatter_dimension=0, til...  286 us
    all_gather x2, waiting for transfers between devices, micro_step(): grad_full = lax.all_gather(rows_grad, 'tensor', axis=0, tiled=True)  165 us
    all_gather x2, waiting for transfers between devices, micro_step(): lax.all_gather(normed_one.astype(jnp.bfloat16), 'tensor', axis=0, tiled=T...  149 us
    unnamed x2, blocking collectives  123 us
    all_gather x2, waiting for transfers between devices, current_set(): lax.all_gather(shard_set[0], 'dp', axis=0, tiled=True)  93.9 us
    dynamic_update_slice x8, local copies, waits for them, and re-layouts, micro_step(): lax.scan(back_block, (zero_heads, zero_heads), (starts, lse_blocks))  92.7 us
    reduce_scatter x2, waiting for transfers between devices, micro_step(): lax.psum_scatter(grad_first, 'tensor', scatter_dimension=0, tiled=True)  79.3 us
  transfers between devices with their start and end apart: 30, of which 19 were waited for; matrix products, arithmetic and copies ran while one was open for 30% of the time, Pallas kernels for 0%

commit v1 on v0

--- a/solution.py
+++ b/solution.py
@@ -131,6 +131,34 @@
     small_zero = tuple((jnp.zeros((width,), jnp.float32) for index_slot in range(6)))
 
     def micro_step(totals, item):
+
+        def _lay_sources_all(work_x):
+            along_axis = "tensor"
+            tall = lax.axis_size(along_axis)
+            extra = lax.axis_index(along_axis)
+            ready, side_arr, piece_next = (tall, extra, work_x.shape[0])
+            copies = [dev * ready if q == 0 else dev for q, dev in enumerate(work_x.shape)]
+            part_now = jnp.zeros(copies, work_x.dtype)
+            even = lax.dynamic_update_slice_in_dim(part_now, work_x, side_arr * piece_next, axis=0)
+            q_next = prior = work_x
+            for nth in tuple(range(1, ready // 2 + 1)):
+                q_next = lax.ppermute(
+                    q_next, axis_name=along_axis, perm=[(q, (q + 1) % ready) for q in range(ready)]
+                )
+                even = lax.dynamic_update_slice_in_dim(
+                    even, q_next, (side_arr - nth) % ready * piece_next, axis=0
+                )
+                if 2 * nth < ready:
+                    prior = lax.ppermute(
+                        prior,
+                        axis_name=along_axis,
+                        perm=[(q, (q - 1) % ready) for q in range(ready)],
+                    )
+                    even = lax.dynamic_update_slice_in_dim(
+                        even, prior, (side_arr + nth) % ready * piece_next, axis=0
+                    )
+            return even
+
         weight_totals, small_totals = totals
         rows_in, rows_grad, seq_length = item
         qkv_full, qkv_shift, dense_full, fc1_full, fc1_shift, fc2_full = current_set()
@@ -179,7 +207,7 @@
         branch = lax.psum_scatter(attn_part + ffn_part, "tensor", scatter_dimension=0, tiled=True)
         output_rows = (residual + branch + dense_shift + fc2_shift).astype(jnp.bfloat16)
         back_set = current_set()
-        grad_full = lax.all_gather(rows_grad, "tensor", axis=0, tiled=True)
+        grad_full = _lay_sources_all(rows_grad)
         grad_dense = jnp.einsum("lhe,ld->hed", mixed, grad_full, preferred_element_type=jnp.float32)
         grad_mixed = jnp.einsum(
             "ld,hed->lhe", grad_full, back_set[2], preferred_element_type=jnp.float32

time: 2310 us -> 2220 us (0.961)
  waiting for transfers between devices: 1340 us -> 1200 us
  starting transfers between devices: 18.6 us -> 51.4 us
    all_gather x2 -> x0, waiting for transfers between devices: 165 us -> none  [micro_step(): grad_full = lax.all_gather(rows_grad, 'tensor', axis=0, tiled=True)]
    ppermute x0 -> x6, waiting for transfers between devices: none -> 142 us  [the longest x2 88.1 us: _lay_sources_all(): lax.ppermute(prior, axis_name=along_axis, perm=[(q, (q - 1) % ready) for...]
    all_gather x2, waiting for transfers between devices: 149 us -> 47.3 us  [micro_step(): lax.all_gather(normed_one.astype(jnp.bfloat16), 'tensor', axis=0, tiled=T...]
    ppermute x0 -> x6, starting transfers between devices: none -> 32.9 us  [the longest x4 26.8 us: _lay_sources_all(): lax.ppermute(q_next, axis_name=along_axis, perm=[(q, (q + 1) % ready) for...]
  transfers between devices with their start and end apart: 30 -> 34, of which waited for: 19 -> 21; matrix products, arithmetic and copies ran while one was open for 30% -> 32% of each run, Pallas kernels for 0% -> 0%
where the time goes in v1:
time: 2220 us; the launch traced here: 2210 us
  waiting for transfers between devices  1200 us (54%)
  matrix products  387 us (17%)
  local copies, waits for them, and re-layouts  256 us (12%)
  blocking collectives  159 us (7%)
  other arithmetic  110 us (5%)
  starting transfers between devices  51.4 us (2%)
  loops' own time  25.3 us (1%)
    reduce_scatter x2, waiting for transfers between devices, micro_step(): lax.psum_scatter(grad_second, 'tensor', scatter_dimension=0, tiled=True)  295 us
    reduce_scatter x2, waiting for transfers between devices, micro_step(): lax.psum_scatter(attn_part + ffn_part, 'tensor', scatter_dimension=0, til...  287 us
    unnamed x2, blocking collectives  123 us
    all_gather x2, waiting for transfers between devices, current_set(): lax.all_gather(shard_set[0], 'dp', axis=0, tiled=True)  96.6 us
    dynamic_update_slice x8, local copies, waits for them, and re-layouts, micro_step(): lax.scan(back_block, (zero_heads, zero_heads), (starts, lse_blocks))  92.9 us
    ppermute x2, waiting for transfers between devices, _lay_sources_all(): lax.ppermute(prior, axis_name=along_axis, perm=[(q, (q - 1) % ready) for...  88.1 us
    reduce_scatter x2, waiting for transfers between devices, micro_step(): lax.psum_scatter(grad_first, 'tensor', scatter_dimension=0, tiled=True)  79.6 us
    reduce_scatter x1, waiting for transfers between devices, per_device(): lax.psum_scatter(weight_totals[5].astype(jnp.bfloat16), 'dp', scatter_dim...  72.2 us
  transfers between devices with their start and end apart: 34, of which 21 were waited for; matrix products, arithmetic and copies ran while one was open for 32% of the time, Pallas kernels for 0%

profile of v1, /device:TPU:0, one launch (start us, length us, event | category | flops | bytes accessed | tf_op | source)
XLA Modules:
  0.0 2209.2 jit_solution(6585401585072268613)
XLA Ops:
  28.8 23.3 %all-to-all-done = bf16[2,8,32,2048]{3,2,0,1:T(8,128)(2,1)S(1)} async-done(((bf16[2,8,32,2048]{3,2,0,1:T(8,128)(2,1)}), bf16[2,8,32,2048]{3,2,0,1:T(8,128)(2,1)S(1)}, u32[]{:S(2)}, u32[]{:S(2)}) %all-to-all-start) | async-done | bytes 2097184 | tf_op jit(solution)/shard_map/all_to_all | solution.py:88
  58.2 58.6 %all-reduce.14 = (bf16[2048]{0:T(1024)(128)(2,1)S(1)}, bf16[2048]{0:T(1024)(128)(2,1)S(1)}, bf16[2048]{0:T(1024)(128)(2,1)S(1)}, bf16[2048]{0:T(1024)(128)(2,1)S...) all-reduce(bf16[2048]{0:T(1024)(128)(2,1)S(1)} %dynamic-update-slic, ...), channel_id=1, replica_groups=mesh['dp'=8,'tensor'=4] {'dp','tensor'}, use_global_device_ids=true, to_apply=%add | all-reduce | flops 12288 | bytes 49152
  127.9 1681.2 %while.108 = (s32[]{:T(128)}, f32[2048,2,768]{2,0,1:T(8,128)}, f32[2,768]{1,0:T(2,128)}, f32[2,256,2048]{2,1,0:T(8,128)}, f32[2048,2048]{1,0:T(8,128)}, /*index=...) while((s32[]{:T(128)}, f32[2048,2,768]{2,0,1:T(8,128)}, ...), condition=%wide.region_24.26_spmd.clone.clone.clone.clone, body=%wide.region_0.25_spmd.clone.clone.clone.clone.sunk | while | flops 81338195968 | bytes 873498304 | solution.py:308
  170.9 58.8 %collective-permute-done.1 = bf16[256,2048]{1,0:T(8,128)(2,1)} collective-permute-done((bf16[256,2048]{1,0:T(8,128)(2,1)S(1)}, bf16[256,2048]{1,0:T(8,128)(2,1)}, u32[]{:S(2)}, u32[]{:S(2)}) %collective-permute-start.1) | collective-permute-done | bytes 1048608 | tf_op jit(solution)/shard_map/while/body/eval_jaxpr/ppermute | solution.py:152
  274.0 48.3 %all-gather.13.cloned.1.call-done = bf16[2048,2,768]{0,2,1:T(8,128)(2,1)} async-done(((bf16[256,2,768]{0,2,1:T(8,128)(2,1)}), bf16[2048,2,768]{0,2,1:T(8,128)(2,1)}) %all-gather.13.cloned.1.call-update) | async-done | bytes 6291472 | tf_op jit(solution)/shard_map/while/body/eval_jaxpr/all_gather | solution.py:106
  359.6 87.4 %while.110 = (s32[]{:T(128)}, f32[1024,2,256]{0,2,1:T(8,128)}, f32[1024,2,256]{0,2,1:T(8,128)}, f32[2,512,2,256]{1,0,3,2:T(2,128)}, s32[2]{0:T(128)S(1)}, /*inde...) while((s32[]{:T(128)}, f32[1024,2,256]{0,2,1:T(8,128)}, ...), condition=%wide.region_9.10_spmd.clone.clone, body=%wide.region_7.9_spmd.clone.clone.sunk | while | flops 2704015360 | bytes 111194568 | solution.py:269
  492.7 31.3 %fusion.251 = (bf16[1024,2048]{1,0:T(8,128)(2,1)}, f32[1024,2048]{1,0:T(8,128)}) fusion(f32[2048]{0:T(1024)S(1)} %bitcast.324, bf16[1024,2048]{1,0:T(8,128)(2,1)} %all-gather.19.cloned.1.call-done, bf16[2048,2048]{1,0:T(8,128)(2,1)} %all-gather.21.cloned.1.call-done), kind=kOutput, calls=%fused_computation.67.clone.1 | convolution fusion | flops 8728346624 | bytes 25174016 | tf_op jit(solution)/shard_map/while/body/eval_jaxpr/dot_general | solution.py:202
  619.4 44.9 %reduce-scatter.25.cloned.1.call-done = f32[256,2048]{1,0:T(8,128)} async-done(((f32[1024,2048]{1,0:T(8,128)}), f32[256,2048]{1,0:T(8,128)}) %reduce-scatter.25.cloned.1.call-update) | async-done | bytes 2097168 | tf_op jit(solution)/shard_map/while/body/eval_jaxpr/reduce_scatter | solution.py:287
  664.3 147.6 %reduce-scatter.23.cloned.1.call-done = f32[256,2048]{1,0:T(8,128)} async-done(((f32[1024,2048]{1,0:T(8,128)}), f32[256,2048]{1,0:T(8,128)}) %reduce-scatter.23.cloned.1.call-update) | async-done | bytes 2097168 | tf_op jit(solution)/shard_map/while/body/eval_jaxpr/reduce_scatter | solution.py:288
  816.1 143.4 %reduce-scatter.27.cloned.1.call-done = f32[256,2048]{1,0:T(8,128)} async-done(((f32[1024,2048]{1,0:T(8,128)}), f32[256,2048]{1,0:T(8,128)}) %reduce-scatter.27.cloned.1.call-update) | async-done | bytes 2097168 | tf_op jit(solution)/shard_map/while/body/eval_jaxpr/reduce_scatter | solution.py:207
  1001.0 24.7 %collective-permute-start.2 = (bf16[256,2048]{1,0:T(8,128)(2,1)S(1)}, bf16[256,2048]{1,0:T(8,128)(2,1)S(1)}, u32[]{:S(2)}, u32[]{:S(2)}) collective-permute-start(bf16[256,2048]{1,0:T(8,128)(2,1)S(1)} %collective-permute-done), channel_id=1, source_target_pairs={{0,1},{1,2},{2,3},{3,0},{4,5},{5,6},{6,7},{7,4},{8,9},{9,10},{10,1... | collective-permute-start | bytes 3145736 | tf_op jit(solution)/shard_map/while/body/eval_jaxpr/ppermute | solution.py:145
  1031.5 29.3 %collective-permute-done.1 = bf16[256,2048]{1,0:T(8,128)(2,1)} collective-permute-done((bf16[256,2048]{1,0:T(8,128)(2,1)S(1)}, bf16[256,2048]{1,0:T(8,128)(2,1)}, u32[]{:S(2)}, u32[]{:S(2)}) %collective-permute-start.1) | collective-permute-done | bytes 1048608 | tf_op jit(solution)/shard_map/while/body/eval_jaxpr/ppermute | solution.py:152
  1087.4 25.2 %all-gather.15.cloned.1.call-done = bf16[1024,2048]{1,0:T(8,128)(2,1)} async-done(((bf16[256,2048]{1,0:T(8,128)(2,1)}), bf16[1024,2048]{1,0:T(8,128)(2,1)}) %all-gather.15.cloned.1.call-update) | async-done | bytes 4194320 | tf_op jit(solution)/shard_map/while/body/eval_jaxpr/all_gather | solution.py:169
  1112.6 48.3 %all-gather.13.cloned.1.call-done = bf16[2048,2,768]{0,2,1:T(8,128)(2,1)} async-done(((bf16[256,2,768]{0,2,1:T(8,128)(2,1)}), bf16[2048,2,768]{0,2,1:T(8,128)(2,1)}) %all-gather.13.cloned.1.call-update) | async-done | bytes 6291472 | tf_op jit(solution)/shard_map/while/body/eval_jaxpr/all_gather | solution.py:106
  1198.2 87.4 %while.110 = (s32[]{:T(128)}, f32[1024,2,256]{0,2,1:T(8,128)}, f32[1024,2,256]{0,2,1:T(8,128)}, f32[2,512,2,256]{1,0,3,2:T(2,128)}, s32[2]{0:T(128)S(1)}, /*inde...) while((s32[]{:T(128)}, f32[1024,2,256]{0,2,1:T(8,128)}, ...), condition=%wide.region_9.10_spmd.clone.clone, body=%wide.region_7.9_spmd.clone.clone.sunk | while | flops 2704015360 | bytes 111194568 | solution.py:269
  1331.4 31.4 %fusion.251 = (bf16[1024,2048]{1,0:T(8,128)(2,1)}, f32[1024,2048]{1,0:T(8,128)}) fusion(f32[2048]{0:T(1024)S(1)} %bitcast.324, bf16[1024,2048]{1,0:T(8,128)(2,1)} %all-gather.19.cloned.1.call-done, bf16[2048,2048]{1,0:T(8,128)(2,1)} %all-gather.21.cloned.1.call-done), kind=kOutput, calls=%fused_computation.67.clone.1 | convolution fusion | flops 8728346624 | bytes 25174016 | tf_op jit(solution)/shard_map/while/body/eval_jaxpr/dot_general | solution.py:202
  1468.3 34.6 %reduce-scatter.25.cloned.1.call-done = f32[256,2048]{1,0:T(8,128)} async-done(((f32[1024,2048]{1,0:T(8,128)}), f32[256,2048]{1,0:T(8,128)}) %reduce-scatter.25.cloned.1.call-update) | async-done | bytes 2097168 | tf_op jit(solution)/shard_map/while/body/eval_jaxpr/reduce_scatter | solution.py:287
  1503.0 147.4 %reduce-scatter.23.cloned.1.call-done = f32[256,2048]{1,0:T(8,128)} async-done(((f32[1024,2048]{1,0:T(8,128)}), f32[256,2048]{1,0:T(8,128)}) %reduce-scatter.23.cloned.1.call-update) | async-done | bytes 2097168 | tf_op jit(solution)/shard_map/while/body/eval_jaxpr/reduce_scatter | solution.py:288
  1654.6 143.2 %reduce-scatter.27.cloned.1.call-done = f32[256,2048]{1,0:T(8,128)} async-done(((f32[1024,2048]{1,0:T(8,128)}), f32[256,2048]{1,0:T(8,128)}) %reduce-scatter.27.cloned.1.call-update) | async-done | bytes 2097168 | tf_op jit(solution)/shard_map/while/body/eval_jaxpr/reduce_scatter | solution.py:207
  1870.6 22.5 %all-to-all-done.3 = bf16[2,1,256,2048]{3,0,1,2:T(2,128)(2,1)S(1)} async-done(((bf16[2,1,256,2048]{3,0,1,2:T(2,128)(2,1)}), bf16[2,1,256,2048]{3,0,1,2:T(2,128)(2,1)S(1)}, u32[]{:S(2)}, u32[]{:S(2)}) %all-to-all-start.3) | async-done | bytes 2097184 | tf_op jit(solution)/shard_map/all_to_all | solution.py:334
  1899.0 64.1 %all-reduce.13 = (f32[2048]{0:T(1024)S(1)}, f32[2048]{0:T(1024)S(1)}, f32[2048]{0:T(1024)S(1)}, f32[2048]{0:T(1024)S(1)}, f32[2048]{0:T(1024)S(1)}, /*index=5*/f32[2048]{0:T(1024)S(1)}) all-reduce(f32[2048]{0:T(1024)S(1)} %copy-done.34, f32[2048]{0:T(1024)S(1)} %copy-done.37, ...), channel_id=5, replica_groups=mesh['dp'=8,'tensor'=4] {'dp','tensor'}, use_global_device_ids=true, to_apply=%region_26.28.clone | all-reduce | flops 12288 | bytes 98304
  1986.4 62.7 %all-reduce.17.cloned.1.call-done = bf16[2048,2,768]{2,1,0:T(2,128)(2,1)} async-done(((bf16[2048,2,768]{2,1,0:T(2,128)(2,1)}), bf16[2048,2,768]{2,1,0:T(2,128)(2,1)}) %all-reduce.17.cloned.1.call-update) | async-done | bytes 6291472
  2051.9 72.0 %reduce-scatter.15.cloned.1.call-done = bf16[256,2048]{1,0:T(8,128)(2,1)} async-done(((bf16[2048,2048]{1,0:T(8,128)(2,1)}), bf16[256,2048]{1,0:T(8,128)(2,1)}) %reduce-scatter.15.cloned.1.call-update) | async-done | bytes 1048592 | tf_op jit(solution)/shard_map/reduce_scatter | solution.py:321
  2126.6 72.2 %reduce-scatter.17.cloned.1.call-done = bf16[2048,256]{1,0:T(8,128)(2,1)} async-done(((bf16[2048,2048]{1,0:T(8,128)(2,1)}), bf16[2048,256]{1,0:T(8,128)(2,1)}) %reduce-scatter.17.cloned.1.call-update) | async-done | bytes 1048592 | tf_op jit(solution)/shard_map/reduce_scatter | solution.py:327
  (653 shorter events, 868.0 us)
Async XLA Ops:
  128.3 117.4 %all-gather.17.cloned.1.call-start = ((), (), s32[]{:S(2)}) async-start(), calls=%async_computation.20 | async-start | bytes 2359296 | tf_op jit(solution)/shard_map/while/body/eval_jaxpr/all_gather | solution.py:108
  129.0 145.0 %all-gather.15.cloned.1.call-start = ((), (), s32[]{:S(2)}) async-start(), calls=%async_computation.19 | async-start | bytes 5242880 | tf_op jit(solution)/shard_map/while/body/eval_jaxpr/all_gather | solution.py:169
  132.7 189.6 %all-gather.13.cloned.1.call-start = ((), (), s32[]{:S(2)}) async-start(), calls=%async_computation.18 | async-start | bytes 7077888 | tf_op jit(solution)/shard_map/while/body/eval_jaxpr/all_gather | solution.py:106
  133.4 359.3 %all-gather.19.cloned.1.call-start = ((), (), s32[]{:S(2)}) async-start(), calls=%async_computation.21 | async-start | bytes 5242880 | tf_op jit(solution)/shard_map/while/body/eval_jaxpr/all_gather | solution.py:170
  134.0 358.7 %all-gather.21.cloned.1.call-start = ((), (), s32[]{:S(2)}) async-start(), calls=%async_computation.22 | async-start | bytes 9437184 | tf_op jit(solution)/shard_map/while/body/eval_jaxpr/all_gather | solution.py:109
  134.6 389.5 %all-gather.23.cloned.1.call-start = ((), (), s32[]{:S(2)}) async-start(), calls=%async_computation.23 | async-start | bytes 9437184 | tf_op jit(solution)/shard_map/while/body/eval_jaxpr/all_gather | solution.py:111
  140.5 523.8 %reduce-scatter.25.cloned.1.call-start = ((), (), s32[]{:S(2)}) async-start(), calls=%async_computation.25 | async-start | bytes 10485760 | tf_op jit(solution)/shard_map/while/body/eval_jaxpr/reduce_scatter | solution.py:287
  483.3 328.7 %reduce-scatter.23.cloned.1.call-start = ((), (), s32[]{:S(2)}) async-start(), calls=%async_computation.24 | async-start | bytes 10485760 | tf_op jit(solution)/shard_map/while/body/eval_jaxpr/reduce_scatter | solution.py:288
  554.4 405.1 %reduce-scatter.27.cloned.1.call-start = ((), (), s32[]{:S(2)}) async-start(), calls=%async_computation.26 | async-start | bytes 10485760 | tf_op jit(solution)/shard_map/while/body/eval_jaxpr/reduce_scatter | solution.py:207
  964.9 116.2 %all-gather.17.cloned.1.call-start = ((), (), s32[]{:S(2)}) async-start(), calls=%async_computation.20 | async-start | bytes 2359296 | tf_op jit(solution)/shard_map/while/body/eval_jaxpr/all_gather | solution.py:108
  965.5 147.1 %all-gather.15.cloned.1.call-start = ((), (), s32[]{:S(2)}) async-start(), calls=%async_computation.19 | async-start | bytes 5242880 | tf_op jit(solution)/shard_map/while/body/eval_jaxpr/all_gather | solution.py:169
  969.1 191.8 %all-gather.13.cloned.1.call-start = ((), (), s32[]{:S(2)}) async-start(), calls=%async_computation.18 | async-start | bytes 7077888 | tf_op jit(solution)/shard_map/while/body/eval_jaxpr/all_gather | solution.py:106
  969.7 361.7 %all-gather.19.cloned.1.call-start = ((), (), s32[]{:S(2)}) async-start(), calls=%async_computation.21 | async-start | bytes 5242880 | tf_op jit(solution)/shard_map/while/body/eval_jaxpr/all_gather | solution.py:170
  970.5 360.9 %all-gather.21.cloned.1.call-start = ((), (), s32[]{:S(2)}) async-start(), calls=%async_computation.22 | async-start | bytes 9437184 | tf_op jit(solution)/shard_map/while/body/eval_jaxpr/all_gather | solution.py:109
  971.0 391.8 %all-gather.23.cloned.1.call-start = ((), (), s32[]{:S(2)}) async-start(), calls=%async_computation.23 | async-start | bytes 9437184 | tf_op jit(solution)/shard_map/while/body/eval_jaxpr/all_gather | solution.py:111
  977.0 526.0 %reduce-scatter.25.cloned.1.call-start = ((), (), s32[]{:S(2)}) async-start(), calls=%async_computation.25 | async-start | bytes 10485760 | tf_op jit(solution)/shard_map/while/body/eval_jaxpr/reduce_scatter | solution.py:287
  1322.0 328.4 %reduce-scatter.23.cloned.1.call-start = ((), (), s32[]{:S(2)}) async-start(), calls=%async_computation.24 | async-start | bytes 10485760 | tf_op jit(solution)/shard_map/while/body/eval_jaxpr/reduce_scatter | solution.py:288
  1393.2 404.6 %reduce-scatter.27.cloned.1.call-start = ((), (), s32[]{:S(2)}) async-start(), calls=%async_computation.26 | async-start | bytes 10485760 | tf_op jit(solution)/shard_map/while/body/eval_jaxpr/reduce_scatter | solution.py:207
  1809.1 157.4 %reduce-scatter.19.cloned.1.call-start = ((), (), s32[]{:S(2)}) async-start(), calls=%async_computation.15 | async-start | bytes 221184
  1810.8 157.2 %reduce-scatter.21.cloned.1.call-start = ((), (), s32[]{:S(2)}) async-start(), calls=%async_computation.16 | async-start | bytes 294912
  1812.4 171.9 %reduce-scatter.13.cloned.1.call-start = ((), (), s32[]{:S(2)}) async-start(), calls=%async_computation.12 | async-start | bytes 2359296 | tf_op jit(solution)/shard_map/reduce_scatter | solution.py:318
  1816.3 232.7 %all-reduce.17.cloned.1.call-start = ((), (), s32[]{:S(2)}) async-start(), calls=%async_computation.17 | async-start | bytes 12582912
  1838.3 285.5 %reduce-scatter.15.cloned.1.call-start = ((), (), s32[]{:S(2)}) async-start(), calls=%async_computation.13 | async-start | bytes 9437184 | tf_op jit(solution)/shard_map/reduce_scatter | solution.py:321
  1847.5 351.4 %reduce-scatter.17.cloned.1.call-start = ((), (), s32[]{:S(2)}) async-start(), calls=%async_computation.14 | async-start | bytes 9437184 | tf_op jit(solution)/shard_map/reduce_scatter | solution.py:327
  (147 other events, 8305.1 us)
Sparse Core Ops, SparseCore 0:
  131.0 26.9 all-gather.16
  159.6 114.3 all-gather.14
  275.8 46.3 all-gather.12
  324.2 80.7 all-gather.18
  406.8 52.9 all-gather.20
  461.5 55.9 all-gather.22
  519.8 144.4 reduce-scatter.24
  666.7 145.2 reduce-scatter.22
  814.3 145.1 reduce-scatter.26
  967.3 28.6 all-gather.16
  997.5 115.0 all-gather.14
  1114.3 46.5 all-gather.12
  1163.0 80.7 all-gather.18
  1245.6 52.9 all-gather.20
  1300.2 55.9 all-gather.22
  1358.4 144.4 reduce-scatter.24
  1505.2 145.1 reduce-scatter.22
  1652.6 145.1 reduce-scatter.26
Sparse Core Ops, SparseCore 1:
  1813.2 34.2 reduce-scatter.18
  1851.3 34.6 reduce-scatter.20
  1889.1 51.9 reduce-scatter.12
  1944.7 104.3 all-reduce.16
  2052.6 71.2 reduce-scatter.14
  2127.7 71.1 reduce-scatter.16
